TPU v7x, 256 devices: a whole 4x4x8 slice. The times are simulated.
256 devices in a mesh: lon: 16 (over y, z_lo, core), lat: 16 (over x, z_hi).
Axes of the slice: x: 4, y: 4, z: 8 (z_hi: 4, z_lo: 2; z = z_hi * 2 + z_lo), core: 2. Of those that a mesh axis runs over, the one named last changes fastest.
Arguments:
- fine_state: bfloat16 [2048, 1024, 128], P('lon', 'lat'), may hold values from -6 to 6
- coarse_state: bfloat16 [128, 64, 512], P('lon', 'lat'), may hold values from -6 to 6
- norm_gains: float32 [2, 128], replicated, may hold values from 0.25 to 1.75
- kernels: bfloat16 [2, 3, 3, 128, 128], replicated, may hold values from -0.1875 to 0.1875
- token_gain: float32 [512], replicated, may hold values from 0.25 to 1.75
- head_gains: float32 [2, 64], replicated, may hold values from 1.2 to 2.2
- query_weight: bfloat16 [512, 512], replicated, may hold values from -0.25 to 0.25
- keyvalue_weight: bfloat16 [512, 1024], replicated, may hold values from -0.25 to 0.25
- output_weight: bfloat16 [512, 512], replicated, may hold values from -0.25 to 0.25
- expand_weight: bfloat16 [512, 128], replicated, may hold values from -0.25 to 0.25
Outputs:
- fine_result: bfloat16 [2048, 1024, 128], P('lon', 'lat')
- coarse_result: bfloat16 [128, 64, 512], P('lon', 'lat')
All inputs are finite; a program needn't handle non-finite values.
Results may differ from a plain program's by a relative error of at most 0.005.
Values may be sent and summed in bfloat16 or wider, within the bound.
No kernel may reach another device: no remote copies, remote signals or barrier semaphores. Data moves between devices by JAX's collectives and lax.ppermute only.
A program may use at most 192 MiB of HBM per device.

v0:
```python
import math
import jax
import jax.numpy as jnp
from jax import lax
from jax.sharding import PartitionSpec as P


def padded_2(block, sides, width, periodic):
    for axis, dim in sides:
        count = lax.axis_size(axis)
        forward = [(i, i + 1) for i in range(count - 1)]
        if periodic:
            forward.append((count - 1, 0))
        backward = [(target, source) for source, target in forward]
        low = lax.ppermute(
            lax.slice_in_dim(block, block.shape[dim] - width, None, axis=dim), axis, forward
        )
        high = lax.ppermute(lax.slice_in_dim(block, 0, width, axis=dim), axis, backward)
        block = jnp.concatenate([low, block, high], axis=dim)
    return block


def rescale_rows(matrix, gain_row):
    return matrix * lax.rsqrt(jnp.mean(matrix * matrix, axis=-1, keepdims=True) + 1e-06) * gain_row


def rescale_heads(projected, gain_row):
    shaped = projected.reshape(projected.shape[0], -1, gain_row.shape[0])
    return rescale_rows(shaped, gain_row)


def convolve(padded, kernel):
    return lax.conv_general_dilated(
        padded[None],
        kernel,
        (1, 1),
        "VALID",
        dimension_numbers=("NHWC", "HWIO", "NHWC"),
        preferred_element_type=jnp.float32,
    )[0]


def attach_rims(hidden, rim_width):
    wrapped = padded_2(hidden, (("lon", 0),), rim_width, True)
    return padded_2(wrapped, (("lat", 1),), rim_width, False)


def local(
    fine_state,
    coarse_state,
    norm_gains,
    kernels,
    token_gain,
    head_gains,
    query_weight,
    keyvalue_weight,
    output_weight,
    expand_weight,
):
    width_all = query_weight.shape[0]
    head_size = head_gains.shape[1]
    head_count = width_all // head_size
    lon_tokens = coarse_state.shape[0]
    lat_tokens = coarse_state.shape[1]
    lon_cells, lat_cells, channels = fine_state.shape
    first_hidden = jax.nn.silu(rescale_rows(fine_state.astype(jnp.float32), norm_gains[0])).astype(
        jnp.bfloat16
    )
    first_output = convolve(attach_rims(first_hidden, 1), kernels[0])
    second_hidden = jax.nn.silu(rescale_rows(first_output, norm_gains[1])).astype(jnp.bfloat16)
    second_output = convolve(attach_rims(second_hidden, 1), kernels[1])
    tokens = coarse_state.reshape(-1, width_all)
    normed = rescale_rows(tokens.astype(jnp.float32), token_gain).astype(jnp.bfloat16)
    scale_factor = 1.0 / math.sqrt(head_size)
    queries = (
        rescale_heads(
            jnp.dot(normed, query_weight, preferred_element_type=jnp.float32), head_gains[0]
        )
        * scale_factor
    ).astype(jnp.bfloat16)
    projected = jnp.dot(normed, keyvalue_weight, preferred_element_type=jnp.float32)
    key_rows = (
        rescale_heads(projected[:, :width_all], head_gains[1])
        .astype(jnp.bfloat16)
        .reshape(-1, width_all)
    )
    value_rows = projected[:, width_all:].astype(jnp.bfloat16)
    key_rows, value_rows = (key_rows, value_rows)
    accumulate_key_rows = lax.all_gather(key_rows, ("lon", "lat"), axis=0, tiled=True)
    accumulate_value_rows = lax.all_gather(value_rows, ("lon", "lat"), axis=0, tiled=True)
    key_heads = accumulate_key_rows.reshape(accumulate_key_rows.shape[0], head_count, head_size)
    value_heads = accumulate_value_rows.reshape(
        accumulate_value_rows.shape[0], head_count, head_size
    )
    scores = jnp.einsum("thd,shd->hts", queries, key_heads, preferred_element_type=jnp.float32)
    weights = jnp.exp(scores)
    totals = jnp.sum(weights, axis=-1)
    summed = jnp.einsum(
        "hts,shd->thd",
        weights.astype(jnp.bfloat16),
        value_heads,
        preferred_element_type=jnp.float32,
    )
    summed, totals = (summed, totals)
    attended = (
        (summed / jnp.transpose(totals)[:, :, None]).reshape(-1, width_all).astype(jnp.bfloat16)
    )
    coarse_result = (
        tokens.astype(jnp.float32)
        + jnp.dot(attended, output_weight, preferred_element_type=jnp.float32)
    ).astype(jnp.bfloat16)
    lifted = jnp.dot(coarse_result, expand_weight, preferred_element_type=jnp.float32).reshape(
        lon_tokens, 1, lat_tokens, 1, channels
    )
    merged = (fine_state.astype(jnp.float32) + second_output).reshape(
        lon_tokens, lon_cells // lon_tokens, lat_tokens, lat_cells // lat_tokens, channels
    ) + lifted
    fine_result = merged.reshape(lon_cells, lat_cells, channels).astype(jnp.bfloat16)
    return (fine_result, coarse_result.reshape(lon_tokens, lat_tokens, width_all))


def solution(mesh):
    return jax.shard_map(
        local,
        mesh=mesh,
        in_specs=(
            P("lon", "lat", None),
            P("lon", "lat", None),
            P(),
            P(),
            P(),
            P(),
            P(),
            P(),
            P(),
            P(),
        ),
        out_specs=(P("lon", "lat", None), P("lon", "lat", None)),
        check_vma=False,
    )
```

profile of v0, /device:TPU:99, one launch (start us, length us, event | category | flops | bytes accessed | tf_op | source)
XLA Modules:
  0.0 1499.1 jit_solution(16317238744384808810)
XLA Ops:
  7.2 0.8 reshape.112
  8.1 0.9 multiply_reduce_fusion.2
  8.9 0.1 rsqrt.47
  9.0 1.0 fusion.51
  10.0 0.1 mul.170
  10.1 0.1 reduce_sum.58
  10.2 0.1 copy.53
  10.3 0.1 copy.54
  10.4 0.1 mul.171
  10.5 0.1 mul.172
  10.6 0.8 slice_bitcast_fusion.3
  11.4 0.1 mul.176
  11.4 0.6 multiply_convert_fusion.3
  12.1 0.0 all-gather.3.cloned.1.call-start
  12.2 0.6 slice.102
  12.8 0.1 all-gather.3.cloned.1.call-update
  12.9 0.8 slice_bitcast_fusion.4
  13.6 3.4 fusion.2
  17.1 3.4 fusion.9
  20.5 0.1 fusion.62
  20.6 0.8 collective-permute-start.1
  21.3 2.0 collective-permute-start
  23.3 1.8 collective-permute-done.1
  25.1 1.9 collective-permute-start.3
  27.0 5.7 collective-permute-start.2
  32.7 0.1 multiply_convert_fusion.4
  32.8 0.2 copy.52
  33.1 1.6 collective-permute-done.2
  34.7 1.7 maximum_bitcast_fusion
  36.4 0.2 pad
  36.6 0.3 copy.46
  36.9 0.1 slice.71
  37.1 0.4 copy-done.8
  37.5 5.7 broadcast_select_fusion.1
  43.2 0.9 copy.47
  44.1 1.2 multiply_reduce_fusion
  45.3 1.5 multiply_convert_fusion
  46.7 0.1 fusion.61
  46.8 1.6 collective-permute-start.5
  48.4 2.2 collective-permute-start.4
  50.6 0.4 multiply_reduce_fusion.1
  51.1 1.2 collective-permute-done.5
  52.4 6.7 collective-permute-start.7
  59.0 2.1 collective-permute-start.6
  61.2 3.5 collective-permute-done.6
  64.7 1.8 maximum_bitcast_fusion.1
  66.5 0.2 pad.2
  66.7 0.3 copy.49
  67.0 0.1 slice.75
  67.1 5.7 broadcast_select_fusion
  72.8 3.0 copy.50
  75.8 665.4 %all-gather.5.cloned.1.call-done = bf16[8192,512]{1,0:T(8,128)(2,1)} async-done(((bf16[32,512]{1,0:T(8,128)(2,1)}), bf16[8192,512]{1,0:T(8,128)(2,1)}) %all-gather.5.cloned.1.call-update) | async-done | bytes 8388624 | tf_op jit(solution)/shard_map/all_gather | solution.py:89
  741.2 12.0 copy.55
  753.2 7.0 fusion.63
  760.2 705.3 %all-gather.3.cloned.1.call-done = bf16[8192,512]{1,0:T(8,128)(2,1)} async-done(((bf16[32,512]{1,0:T(8,128)(2,1)}), bf16[8192,512]{1,0:T(8,128)(2,1)}) %all-gather.3.cloned.1.call-update) | async-done | bytes 8388624 | tf_op jit(solution)/shard_map/all_gather | solution.py:90
  1465.4 11.6 copy.51
  1477.0 6.9 fusion.41
  1484.0 0.1 convert_element_type.65
  1484.1 0.2 fusion.37
  1484.3 0.6 reshape.97
  1485.0 0.1 fusion.64
  1485.1 0.5 add.82
  1485.6 4.0 fusion.11
  1489.6 2.7 copy.58
  (37 shorter events, 0.3 us)
Async XLA Ops:
  7.2 1.9 copy-start
  7.2 734.0 %all-gather.5.cloned.1.call-start = ((), (), s32[]{:S(2)}) async-start(), calls=%async_computation.1 | async-start | bytes 8421376 | tf_op jit(solution)/shard_map/all_gather | solution.py:89
  12.1 1453.3 %all-gather.3.cloned.1.call-start = ((), (), s32[]{:S(2)}) async-start(), calls=%async_computation | async-start | bytes 8421376 | tf_op jit(solution)/shard_map/all_gather | solution.py:90
  13.6 19.1 %copy-start.5 = (bf16[8,4,512]{2,1,0:T(4,128)(2,1)S(1)}, bf16[8,4,512]{2,1,0:T(4,128)(2,1)}, u32[]{:S(2)}) copy-start(bf16[8,4,512]{2,1,0:T(4,128)(2,1)} %param.11) | copy-start | bytes 98308
  13.6 19.1 %copy-start.7 = (f32[512]{0:T(512)S(1)}, f32[512]{0:T(512)}, u32[]{:S(2)}) copy-start(f32[512]{0:T(512)} %param.14) | copy-start | bytes 6148
  13.6 19.2 %copy-start.4 = (bf16[512,512]{1,0:T(8,128)(2,1)S(1)}, bf16[512,512]{1,0:T(8,128)(2,1)}, u32[]{:S(2)}) copy-start(bf16[512,512]{1,0:T(8,128)(2,1)} %param.16) | copy-start | bytes 1572868
  20.6 4.5 collective-permute-start.1
  21.3 3.7 collective-permute-start
  25.1 7.9 collective-permute-start.3
  27.0 7.6 collective-permute-start.2
  36.4 1.1 copy-start.8
  36.4 1.1 copy-start.9
  46.8 5.5 collective-permute-start.5
  48.4 3.9 collective-permute-start.4
  52.4 8.8 collective-permute-start.7
  59.0 5.7 collective-permute-start.6
  1477.0 7.1 copy-start.3
  1477.0 7.9 copy-start.6
  1484.0 1.6 copy-start.2
  1485.6 6.7 copy-start.1
Sparse Core Ops, SparseCore 0:
  12.2 728.9 all-gather.4
  743.6 721.7 all-gather.2
where the time goes:
time: 1500 us
  waiting for transfers between devices  1380 us (92%)
  local copies, waits for them, and re-layouts  37 us (2%)
  matrix products  27 us (2%)
  starting transfers between devices  23 us (2%)
  other arithmetic  18.8 us (1%)
    all_gather x1, waiting for transfers between devices, local(): lax.all_gather(value_rows, ('lon', 'lat'), axis=0, tiled=True)  705 us
    all_gather x1, waiting for transfers between devices, local(): lax.all_gather(key_rows, ('lon', 'lat'), axis=0, tiled=True)  665 us
  transfers between devices with their start and end apart: 10, of which 6 were waited for; matrix products, arithmetic and copies ran while one was open for 3% of the time, Pallas kernels for 0%

commit v1 on v0

--- a/solution.py
+++ b/solution.py
@@ -86,7 +86,10 @@
     )
     value_rows = projected[:, width_all:].astype(jnp.bfloat16)
     key_rows, value_rows = (key_rows, value_rows)
-    accumulate_key_rows = lax.all_gather(key_rows, ("lon", "lat"), axis=0, tiled=True)
+    accumulate_key_rows = jnp.concatenate(
+        lax.all_to_all(jnp.stack([key_rows] * lax.axis_size(("lon", "lat"))), ("lon", "lat"), 0, 0),
+        axis=0,
+    )
     accumulate_value_rows = lax.all_gather(value_rows, ("lon", "lat"), axis=0, tiled=True)
     key_heads = accumulate_key_rows.reshape(accumulate_key_rows.shape[0], head_count, head_size)
     value_heads = accumulate_value_rows.reshape(

time: 1500 us -> 836 us (0.56)
  waiting for transfers between devices: 1380 us -> 678 us
    all_gather x1 -> x0, waiting for transfers between devices: 665 us -> none  [local(): lax.all_gather(key_rows, ('lon', 'lat'), axis=0, tiled=True)]
    all_gather x1, waiting for transfers between devices: 705 us -> 496 us  [local(): lax.all_gather(value_rows, ('lon', 'lat'), axis=0, tiled=True)]
    ppermute x4, waiting for transfers between devices: 5.11 us -> 165 us  [padded_2(): lax.ppermute(lax.slice_in_dim(block, block.shape[dim] - width, None, axis...]
    another operation x0 -> x2, local copies, waits for them, and re-layouts: none -> 25.5 us  [the longest x1 21.2 us: local(): accumulate_key_rows.reshape(accumulate_key_rows.shape[0], head_count, hea...]
    all_to_all x0 -> x1, starting transfers between devices: none -> 15.3 us  [local(): lax.all_to_all(jnp.stack([key_rows] * lax.axis_size(('lon', 'lat'))), ('l...]
  transfers between devices with their start and end apart: 10 -> 10, of which waited for: 6 -> 8; matrix products, arithmetic and copies ran while one was open for 3% -> 8% of each run, Pallas kernels for 0% -> 0%
where the time goes in v1:
time: 836 us; the launch traced here: 830 us
  waiting for transfers between devices  678 us (81%)
  local copies, waits for them, and re-layouts  50 us (6%)
  starting transfers between devices  37.6 us (4%)
  matrix products  33.6 us (4%)
  other arithmetic  16.5 us (2%)
  between operations  14.7 us (2%)
    all_gather x1, waiting for transfers between devices, local(): lax.all_gather(value_rows, ('lon', 'lat'), axis=0, tiled=True)  496 us
    ppermute x4, waiting for transfers between devices, padded_2(): lax.ppermute(lax.slice_in_dim(block, block.shape[dim] - width, None, axis...  165 us
    another operation x1, local copies, waits for them, and re-layouts, local(): accumulate_key_rows.reshape(accumulate_key_rows.shape[0], head_count, hea...  21.2 us
    ppermute x4, waiting for transfers between devices, padded_2(): lax.ppermute(lax.slice_in_dim(block, 0, width, axis=dim), axis, backward)  17 us
  transfers between devices with their start and end apart: 10, of which 8 were waited for; matrix products, arithmetic and copies ran while one was open for 8% of the time, Pallas kernels for 0%

profile of v1, /device:TPU:99, one launch (start us, length us, event | category | flops | bytes accessed | tf_op | source)
XLA Modules:
  0.0 830.2 jit_solution(5702003983773579740)
XLA Ops:
  7.2 0.9 reshape.110
  8.0 0.9 multiply_reduce_fusion.2
  8.9 0.1 rsqrt.47
  9.0 1.0 fusion.56
  10.0 0.1 mul.172
  10.1 0.1 reduce_sum.58
  10.2 0.1 copy.53
  10.3 0.1 copy.54
  10.4 0.1 mul.173
  10.5 0.1 mul.174
  10.6 0.8 slice_bitcast_fusion.3
  11.3 0.1 mul.178
  11.4 4.3 stack.3
  15.7 15.3 %all-to-all-start = ((bf16[256,32,512]{2,1,0:T(8,128)(2,1)}), bf16[256,32,512]{2,1,0:T(8,128)(2,1)}, u32[]{:S(2)}, u32[]{:S(2)}) async-start(bf16[256,32,512]{2,1,0:T(8,128)(2,1)} %stack.3), calls=%async_computation | async-start | bytes 16777216 | tf_op jit(solution)/shard_map/all_to_all | solution.py:90
  31.1 0.6 slice.102
  31.7 0.1 all-gather.2.cloned.1.call-update
  31.8 1.8 fusion.7
  33.6 3.4 fusion.14
  37.1 0.1 fusion.67
  37.2 1.3 collective-permute-start
  38.5 162.9 %collective-permute-done = bf16[1,64,128]{2,0,1:T(2,128)(2,1)S(1)} collective-permute-done((bf16[1,64,128]{2,0,1:T(2,128)(2,1)S(1)}, bf16[1,64,128]{2,0,1:T(2,128)(2,1)S(1)}, u32[]{:S(2)}, u32[]{:S(2)}) %collective-permute-start) | collective-permute-done | bytes 16416 | tf_op jit(solution)/shard_map/ppermute | solution.py:15
  201.4 9.5 %collective-permute-done.1 = bf16[1,64,128]{2,0,1:T(2,128)(2,1)S(1)} collective-permute-done((bf16[1,64,128]{2,0,1:T(2,128)(2,1)S(1)}, bf16[1,64,128]{2,0,1:T(2,128)(2,1)S(1)}, u32[]{:S(2)}, u32[]{:S(2)}) %collective-permute-start.1) | collective-permute-done | bytes 16416 | tf_op jit(solution)/shard_map/ppermute | solution.py:18
  210.9 5.8 collective-permute-start.2
  216.7 2.4 collective-permute-start.3
  219.1 0.1 multiply_convert_fusion.4
  219.2 0.2 copy.52
  219.5 1.4 collective-permute-done.2
  220.9 3.4 collective-permute-done.3
  224.3 1.7 maximum_bitcast_fusion
  226.1 0.2 pad
  226.3 0.3 copy.46
  226.6 0.1 slice.71
  226.8 0.4 copy-done.10
  227.2 5.7 broadcast_select_fusion.1
  232.8 0.9 copy.47
  233.8 1.2 multiply_reduce_fusion
  234.9 1.5 multiply_convert_fusion
  236.4 0.1 fusion.66
  236.5 0.3 collective-permute-start.4
  236.8 0.2 collective-permute-start.5
  237.1 0.4 multiply_reduce_fusion.1
  237.5 0.3 collective-permute-done.4
  237.9 3.2 collective-permute-done.5
  241.1 1.9 collective-permute-start.6
  243.0 10.3 %collective-permute-start.7 = (bf16[130,1,128]{2,0,1:T(8,128)(2,1)S(1)}, bf16[130,1,128]{2,0,1:T(8,128)(2,1)S(1)}, u32[]{:S(2)}, u32[]{:S(2)}) collective-permute-start(bf16[130,1,128]{2,0,1:T(8,128)(2,1)S(1)} %get-tuple-element.9), channel_id=1, source_target_pairs={{1,0},{2,1},{3,2},{4,3},{5,4},{6,5},{7,6},{8,7},{9,8},{10,9},{11,1... | collective-permute-start | bytes 99848 | tf_op jit(solution)/shard_map/ppermute | solution.py:18
  253.3 0.8 collective-permute-done.7
  254.2 1.8 maximum_bitcast_fusion.1
  255.9 0.2 pad.2
  256.1 0.3 copy.49
  256.4 0.1 slice.75
  256.6 5.7 broadcast_select_fusion
  262.3 3.1 copy.50
  265.3 21.2 %reshape_reshape.3 = bf16[8192,8,64]{2,1,0:T(8,128)(2,1)} reshape(bf16[256,32,512]{2,1,0:T(8,128)(2,1)} %all-to-all-done) | data formatting | bytes 16777216 | tf_op jit(solution)/shard_map/reshape;reshape | solution.py:94
  286.6 13.6 %fusion.68 = (f32[8,32]{1,0:T(8,128)S(1)}, bf16[8,32,8192]{2,1,0:T(8,128)(2,1)}) fusion(bf16[8192,8,64]{2,1,0:T(8,128)(2,1)} %reshape_reshape.3, f32[32,8,64]{2,0,1:T(8,128)S(1)} %get-tuple-element.21, f32[64]{0:T(128)S(1)} %get-tuple-element.18, f32[32,8]{0,1:T(8,128)S(1)} %add_rsqrt_fusion.3), kind=kOutput, calls=%fused_computation.90 | convolution fusion | flops 272695040 | bytes 12650752 | tf_op jit(solution)/shard_map/thd,shd->hts/dot_general | solution.py:98
  300.2 496.1 %all-gather.2.cloned.1.call-done = bf16[8192,512]{1,0:T(8,128)(2,1)} async-done(((bf16[32,512]{1,0:T(8,128)(2,1)}), bf16[8192,512]{1,0:T(8,128)(2,1)}) %all-gather.2.cloned.1.call-update) | async-done | bytes 8388624 | tf_op jit(solution)/shard_map/all_gather | solution.py:93
  796.3 11.6 %copy.51 = bf16[8192,512]{0,1:T(8,128)(2,1)} copy(bf16[8192,512]{1,0:T(8,128)(2,1)} %all-gather.2.cloned.1.call-done) | data formatting | bytes 16777216 | tf_op jit(solution)/shard_map/all_gather | solution.py:93
  807.9 6.9 fusion.46
  814.9 0.1 convert_element_type.66
  815.0 0.2 fusion.42
  815.2 0.6 reshape.95
  815.8 0.1 fusion.69
  816.0 0.5 add.82
  816.5 4.0 fusion.16
  820.5 2.7 copy.58
  (41 shorter events, 0.3 us)
Async XLA Ops:
  7.2 1.8 copy-start
  15.7 16.0 %copy-start.9 = (f32[2,128]{1,0:T(2,128)S(1)}, f32[2,128]{1,0:T(2,128)}, u32[]{:S(2)}) copy-start(f32[2,128]{1,0:T(2,128)} %param.12) | copy-start | bytes 3076
  15.7 16.1 %copy-start.2 = (bf16[128,64,128]{2,1,0:T(8,128)(2,1)S(1)}, bf16[128,64,128]{2,1,0:T(8,128)(2,1)}, u32[]{:S(2)}) copy-start(bf16[128,64,128]{2,1,0:T(8,128)(2,1)} %param.10) | copy-start | bytes 6291460
  15.7 249.6 %all-to-all-start = ((bf16[256,32,512]{2,1,0:T(8,128)(2,1)}), bf16[256,32,512]{2,1,0:T(8,128)(2,1)}, u32[]{:S(2)}, u32[]{:S(2)}) async-start(bf16[256,32,512]{2,1,0:T(8,128)(2,1)} %stack.3), calls=%async_computation | async-start | bytes 16777216 | tf_op jit(solution)/shard_map/all_to_all | solution.py:90
  31.0 765.3 %all-gather.2.cloned.1.call-start = ((), (), s32[]{:S(2)}) async-start(), calls=%async_computation.1 | async-start | bytes 8421376 | tf_op jit(solution)/shard_map/all_gather | solution.py:93
  31.8 187.3 %copy-start.6 = (bf16[8,4,512]{2,1,0:T(4,128)(2,1)S(1)}, bf16[8,4,512]{2,1,0:T(4,128)(2,1)}, u32[]{:S(2)}) copy-start(bf16[8,4,512]{2,1,0:T(4,128)(2,1)} %param.11) | copy-start | bytes 98308
  31.8 187.3 %copy-start.8 = (f32[512]{0:T(512)S(1)}, f32[512]{0:T(512)}, u32[]{:S(2)}) copy-start(f32[512]{0:T(512)} %param.14) | copy-start | bytes 6148
  31.8 187.4 %copy-start.5 = (bf16[512,512]{1,0:T(8,128)(2,1)S(1)}, bf16[512,512]{1,0:T(8,128)(2,1)}, u32[]{:S(2)}) copy-start(bf16[512,512]{1,0:T(8,128)(2,1)} %param.16) | copy-start | bytes 1572868
  37.2 164.2 %collective-permute-start = (bf16[1,64,128]{2,0,1:T(2,128)(2,1)S(1)}, bf16[1,64,128]{2,0,1:T(2,128)(2,1)S(1)}, u32[]{:S(2)}, u32[]{:S(2)}) collective-permute-start(bf16[1,64,128]{2,0,1:T(2,128)(2,1)S(1)} %get-tuple-element.14), channel_id=1, source_target_pairs={{0,16},{16,32},{32,48},{48,64},{64,80},{80,96},{96,112},{112,128},... | collective-permute-start | bytes 49160 | tf_op jit(solution)/shard_map/ppermute | solution.py:15
  38.5 172.4 %collective-permute-start.1 = (bf16[1,64,128]{2,0,1:T(2,128)(2,1)S(1)}, bf16[1,64,128]{2,0,1:T(2,128)(2,1)S(1)}, u32[]{:S(2)}, u32[]{:S(2)}) collective-permute-start(bf16[1,64,128]{2,0,1:T(2,128)(2,1)S(1)} %get-tuple-element.15), channel_id=1, source_target_pairs={{16,0},{32,16},{48,32},{64,48},{80,64},{96,80},{112,96},{128,112},... | collective-permute-start | bytes 49160 | tf_op jit(solution)/shard_map/ppermute | solution.py:18
  210.9 10.0 %collective-permute-start.2 = (bf16[130,1,128]{2,0,1:T(8,128)(2,1)S(1)}, bf16[130,1,128]{2,0,1:T(8,128)(2,1)S(1)}, u32[]{:S(2)}, u32[]{:S(2)}) collective-permute-start(bf16[130,1,128]{2,0,1:T(8,128)(2,1)S(1)} %get-tuple-element.10), channel_id=1, source_target_pairs={{0,1},{1,2},{2,3},{3,4},{4,5},{5,6},{6,7},{7,8},{8,9},{9,10},{10,1... | collective-permute-start | bytes 99848 | tf_op jit(solution)/shard_map/ppermute | solution.py:15
  216.7 7.6 collective-permute-start.3
  226.1 1.1 copy-start.10
  226.1 1.1 copy-start.11
  236.5 1.4 collective-permute-start.4
  236.8 4.2 collective-permute-start.5
  241.1 12.2 %collective-permute-start.6 = (bf16[130,1,128]{2,0,1:T(8,128)(2,1)S(1)}, bf16[130,1,128]{2,0,1:T(8,128)(2,1)S(1)}, u32[]{:S(2)}, u32[]{:S(2)}) collective-permute-start(bf16[130,1,128]{2,0,1:T(8,128)(2,1)S(1)} %get-tuple-element.8), channel_id=1, source_target_pairs={{0,1},{1,2},{2,3},{3,4},{4,5},{5,6},{6,7},{7,8},{8,9},{9,10},{10,1... | collective-permute-start | bytes 99848 | tf_op jit(solution)/shard_map/ppermute | solution.py:15
  243.0 11.1 %collective-permute-start.7 = (bf16[130,1,128]{2,0,1:T(8,128)(2,1)S(1)}, bf16[130,1,128]{2,0,1:T(8,128)(2,1)S(1)}, u32[]{:S(2)}, u32[]{:S(2)}) collective-permute-start(bf16[130,1,128]{2,0,1:T(8,128)(2,1)S(1)} %get-tuple-element.9), channel_id=1, source_target_pairs={{1,0},{2,1},{3,2},{4,3},{5,4},{6,5},{7,6},{8,7},{9,8},{10,9},{11,1... | collective-permute-start | bytes 99848 | tf_op jit(solution)/shard_map/ppermute | solution.py:18
  807.9 7.1 copy-start.4
  807.9 7.9 copy-start.7
  814.8 1.6 copy-start.3
  816.5 6.7 copy-start.1
Sparse Core Ops, SparseCore 0:
  34.3 761.9 all-gather.1
